TPU v7x, 32 devices: a whole 2x2x4 slice. The times are simulated.
32 devices in a mesh: ctx: 8 (over y, x, core), fsdp: 4 (over z).
Axes of the slice: x: 2, y: 2, z: 4, core: 2. Of those that a mesh axis runs over, the one named last changes fastest.
Arguments:
- loaded: bfloat16 [8, 8, 128, 4096], P('ctx', None, None, 'fsdp'), may hold values from -6 to 6
- slot_pos: int32 [8, 8, 128], P('ctx'), may hold values from -1 to 255, as said below
- contig_lengths: int32 [16], replicated, may hold values from 1 to 1024, 2048 in all
- w_in: bfloat16 [4096, 3, 4096], P('ctx', None, 'fsdp'), may hold values from -0.09375 to 0.09375
- short_taps: float32 [3, 7, 4096], P(None, None, 'fsdp'), may hold values from -2 to 2
- long_taps: float32 [128, 4096], P(None, 'fsdp'), may hold values from -0.5 to 0.5
- grad_out: bfloat16 [2048, 4096], P('ctx', 'fsdp'), may hold values from -0.59765625 to 0.59765625
Outputs:
- gated_out: bfloat16 [2048, 4096], P('ctx', 'fsdp')
- token_grads: bfloat16 [2048, 4096], P('ctx', 'fsdp')
- weight_grads: bfloat16 [4096, 3, 4096], P('ctx', None, 'fsdp')
- short_grads: float32 [3, 7, 4096], P(None, None, 'fsdp')
- long_grads: float32 [128, 4096], P(None, 'fsdp')
Inputs may be any that keep to these rules, and one draw needn't show every extreme that they name: `slot_pos`: for each destination e, the slots with a value of 0 or more name every row 0 to 255 of e's block exactly once; -1 marks an empty slot; for each destination some loader fills all 128 of its slots. `contig_lengths`: the lengths sum to 2048.
All inputs are finite; a program needn't handle non-finite values.
Results may differ from a plain program's by a relative error of at most 0.012.
Values may be sent and summed in bfloat16 or wider, within the bound.
A program may use at most 192 MiB of HBM per device.

v0:
```python
import jax
import jax.numpy as jnp
from jax import lax
from jax.sharding import PartitionSpec as P


def passed_along(x, axis, by):
    size = lax.axis_size(axis)
    pairs = [(i, i + by) for i in range(size) if 0 <= i + by < size]
    return lax.ppermute(x, axis, pairs)


def starts_of(positions, contig_lengths):
    ends = jnp.cumsum(contig_lengths, dtype=jnp.int32)
    begins = ends - contig_lengths
    chosen = jnp.where(begins[None, :] <= positions[:, None], begins[None, :], 0)
    return jnp.max(chosen, axis=1)


def lead_filter(ext, taps, positions, begins_here):
    width = taps.shape[0]
    count = ext.shape[0] - width + 1
    bcast_shape = (count,) + (1,) * (ext.ndim - 1)
    total = jnp.zeros((count,) + ext.shape[1:], jnp.float32)
    for tap_index in range(width):
        keep_mask = (positions - tap_index >= begins_here).astype(jnp.float32).reshape(bcast_shape)
        first = width - 1 - tap_index
        total = total + taps[tap_index] * ext[first : first + count] * keep_mask
    return total


def trail_filter(ext, taps, positions, begins_ext):
    width = taps.shape[0]
    count = ext.shape[0] - width + 1
    bcast_shape = (count,) + (1,) * (ext.ndim - 1)
    total = jnp.zeros((count,) + ext.shape[1:], jnp.float32)
    for tap_index in range(width):
        keep_mask = (
            (positions >= begins_ext[tap_index : tap_index + count])
            .astype(jnp.float32)
            .reshape(bcast_shape)
        )
        total = total + taps[tap_index] * ext[tap_index : tap_index + count] * keep_mask
    return total


def tap_sums(grads, ext, width, lead_count, positions, begins_here):
    count = grads.shape[0]
    bcast_shape = (count,) + (1,) * (grads.ndim - 1)
    pieces = []
    for tap_index in range(width):
        keep_mask = (positions - tap_index >= begins_here).astype(jnp.float32).reshape(bcast_shape)
        first = lead_count - tap_index
        pieces.append(jnp.sum(grads * ext[first : first + count] * keep_mask, axis=0))
    return jnp.stack(pieces, 0)


def on_device(loaded, slot_pos, contig_lengths, w_in, short_taps, long_taps, grad_out):
    moved = lax.all_to_all(loaded, "ctx", split_axis=1, concat_axis=0, tiled=True)
    feat_cols = moved.shape[3]
    slot_rows = moved.reshape(-1, feat_cols)
    tok_rows = grad_out.shape[0]
    short_width = short_taps.shape[1]
    long_width = long_taps.shape[0]
    targets = slot_pos.reshape(-1)
    picker = (targets[None, :] == jnp.arange(tok_rows, dtype=jnp.int32)[:, None]).astype(
        jnp.bfloat16
    )
    own_part = jnp.dot(picker, slot_rows, preferred_element_type=jnp.float32).astype(jnp.bfloat16)
    tokens = lax.all_gather(own_part, "fsdp", axis=1, tiled=True)
    gathered = lax.all_gather(w_in, "ctx", axis=0, tiled=True)
    streams = jnp.einsum("td,dsc->tsc", tokens, gathered, preferred_element_type=jnp.float32)
    proj_half = streams.astype(jnp.bfloat16)
    offset = lax.axis_index("ctx") * tok_rows
    positions = offset + jnp.arange(tok_rows, dtype=jnp.int32)
    begins_here = starts_of(positions, contig_lengths)
    short_lags = jnp.transpose(short_taps, (1, 0, 2))
    prev_rows = passed_along(proj_half[tok_rows - (short_width - 1) :], "ctx", 1)
    lead_mixed = jnp.concatenate([prev_rows, proj_half], 0).astype(jnp.float32)
    lead_count = short_width - 1
    filtered = lead_filter(lead_mixed, short_lags, positions, begins_here)
    product = (filtered[:, 1] * filtered[:, 2]).astype(jnp.bfloat16)
    prior_rows = passed_along(product[tok_rows - (long_width - 1) :], "ctx", 1)
    lead_product = jnp.concatenate([prior_rows, product], 0).astype(jnp.float32)
    carried = lead_filter(lead_product, long_taps, positions, begins_here)
    gated_out = (filtered[:, 0] * carried).astype(jnp.bfloat16)
    upstream = grad_out.astype(jnp.float32)
    back_prod = (upstream * filtered[:, 0]).astype(jnp.bfloat16)
    first_grad = upstream * carried
    next_rows = passed_along(back_prod[: long_width - 1], "ctx", -1)
    long_begins = starts_of(
        offset + jnp.arange(tok_rows + long_width - 1, dtype=jnp.int32), contig_lengths
    )
    trail_prod = jnp.concatenate([back_prod, next_rows], 0).astype(jnp.float32)
    grad_product = trail_filter(trail_prod, long_taps, positions, long_begins)
    grad_filtered = jnp.stack(
        [first_grad, grad_product * filtered[:, 2], grad_product * filtered[:, 1]], 1
    ).astype(jnp.bfloat16)
    next_grads = passed_along(grad_filtered[: short_width - 1], "ctx", -1)
    short_begins = starts_of(
        offset + jnp.arange(tok_rows + short_width - 1, dtype=jnp.int32), contig_lengths
    )
    trail_grad = jnp.concatenate([grad_filtered, next_grads], 0).astype(jnp.float32)
    grad_mixed = trail_filter(trail_grad, short_lags, positions, short_begins).astype(jnp.bfloat16)
    long_local = tap_sums(
        back_prod.astype(jnp.float32),
        lead_product,
        long_width,
        long_width - 1,
        positions,
        begins_here,
    )
    short_local = tap_sums(
        grad_filtered.astype(jnp.float32),
        lead_mixed,
        short_width,
        lead_count,
        positions,
        begins_here,
    )
    short_total, long_total = (
        lax.psum(jnp.transpose(short_local, (1, 0, 2)).astype(jnp.bfloat16), "ctx").astype(
            jnp.float32
        ),
        lax.psum(long_local.astype(jnp.bfloat16), "ctx").astype(jnp.float32),
    )
    partial_value = jnp.einsum(
        "tsc,dsc->td", grad_mixed, gathered, preferred_element_type=jnp.float32
    )
    token_grads = lax.psum_scatter(
        partial_value.astype(jnp.bfloat16), "fsdp", scatter_dimension=1, tiled=True
    )
    weight_grads = lax.psum_scatter(
        jnp.einsum("td,tsc->dsc", tokens, grad_mixed, preferred_element_type=jnp.float32).astype(
            jnp.bfloat16
        ),
        "ctx",
        scatter_dimension=0,
        tiled=True,
    )
    return (gated_out, token_grads, weight_grads, short_total, long_total)


def solution(mesh):
    in_specs = (
        P("ctx", None, None, "fsdp"),
        P("ctx", None, None),
        P(),
        P("ctx", None, "fsdp"),
        P(None, None, "fsdp"),
        P(None, "fsdp"),
        P("ctx", "fsdp"),
    )
    out_specs = (
        P("ctx", "fsdp"),
        P("ctx", "fsdp"),
        P("ctx", None, "fsdp"),
        P(None, None, "fsdp"),
        P(None, "fsdp"),
    )
    return jax.shard_map(
        on_device, mesh=mesh, in_specs=in_specs, out_specs=out_specs, check_vma=False
    )
```

profile of v0, /device:TPU:0, one launch (start us, length us, event | category | flops | bytes accessed | tf_op | source)
XLA Modules:
  0.0 702.3 jit_solution(11985297371757299991)
XLA Ops:
  7.2 31.8 %all_to_all.4 = bf16[1,8,128,1024]{3,2,0,1:T(8,128)(2,1)S(1)} all-to-all(bf16[1,8,128,1024]{3,2,0,1:T(8,128)(2,1)} %bitcast.209), channel_id=1, replica_groups=mesh['ctx'=8,'fsdp'=4] {'ctx'}, dimensions={1} | all-to-all | bytes 4194304 | tf_op jit(solution)/shard_map/all_to_all | solution.py:59
  39.0 1.5 convolution_convert_fusion.1
  41.9 0.7 compare_convert_fusion.102
  42.7 0.7 compare_convert_fusion.129
  43.4 0.7 compare_convert_fusion.130
  44.8 0.7 compare_convert_fusion.132
  45.6 0.7 compare_convert_fusion.133
  51.3 1.4 compare_convert_fusion.219
  53.0 33.0 %all-gather.3.cloned.1.call-done = bf16[256,4096]{1,0:T(8,128)(2,1)} async-done(((bf16[256,1024]{1,0:T(8,128)(2,1)}), bf16[256,4096]{1,0:T(8,128)(2,1)}) %all-gather.3.cloned.1.call-update) | async-done | bytes 2097168 | tf_op jit(solution)/shard_map/all_gather | solution.py:70
  86.0 126.0 %all-gather.5.cloned.1.call-done = bf16[4096,3,1024]{2,0,1:T(8,128)(2,1)} async-done(((bf16[512,3,1024]{2,0,1:T(8,128)(2,1)}), bf16[4096,3,1024]{2,0,1:T(8,128)(2,1)}) %all-gather.5.cloned.1.call-update) | async-done | bytes 25165840 | tf_op jit(solution)/shard_map/all_gather | solution.py:71
  212.0 12.2 %fusion.32 = bf16[256,3,1024]{2,0,1:T(8,128)(2,1)S(1)} fusion(bf16[4096,3,1024]{2,0,1:T(8,128)(2,1)} %all-gather.5.cloned.1.call-done, bf16[256,4096]{1,0:T(8,128)(2,1)} %all-gather.3.cloned.1.call-done), kind=kOutput, calls=%fused_computation.177 | convolution fusion | flops 6443237376 | bytes 28835840 | tf_op jit(solution)/shard_map/td,dsc->tsc/dot_general | solution.py:72
  224.2 2.2 collective-permute-start
  227.8 3.6 multiply_add_fusion
  231.7 3.7 collective-permute-start.1
  237.0 3.4 fusion.266
  240.4 0.8 slice.2608
  241.2 1.5 collective-permute-start.2
  242.6 3.3 fusion.268
  245.9 3.3 fusion.270
  249.2 3.3 fusion.272
  252.5 3.3 fusion.274
  255.7 3.1 fusion.276
  258.9 3.3 fusion.278
  262.1 3.3 fusion.280
  265.4 3.3 fusion.282
  268.8 3.3 fusion.284
  272.1 3.3 fusion.286
  275.5 3.5 fusion.288
  279.3 3.3 fusion.290
  283.0 9.1 %multiply_add_fusion.2 = f32[256,1024]{1,0:T(8,128)S(1)} fusion(f32[383,1024]{1,0:T(8,128)S(1)} %maximum_convert_fusion.2, f32[256]{0:T(256)} %copy-done.108, f32[1024]{0:T(1024)S(1)} %bitcast.309, f32[256]{0:T(256)} %copy-done.109, f32[1024]{0:T(1024)S(1)} %bitcast.312, f32[256]{0:T(256)} %copy-done.110, f32[1024]{0:T(1024)S(1)} %bitcast.314, ...), kind=kLoop, calls=%fused_computation.832 | loop fusion | flops 33554432 | bytes 46357504 | tf_op jit(solution)/shard_map/add | solution.py:28
  292.1 19.1 %fusion.550 = (bf16[256,1,1024]{2,0,1:T(8,128)(2,1)}, f32[256,1024]{1,0:T(8,128)}) fusion(bf16[256,1024]{1,0:T(8,128)(2,1)} %param.13, f32[256]{0:T(256)} %get-tuple-element.435, f32[383,1024]{1,0:T(8,128)S(1)} %maximum_convert_fusion.2, f32[1024]{0:T(1024)} %bitcast.279, f32[256]{0:T(256)} %get-tuple-element.436, f32[1024]{0:T(1024)} %bitcast.281, ...), kind=kLoop, calls=%fused_computation.840 | loop fusion | flops 67633152 | bytes 92709888 | tf_op jit(solution)/shard_map/stack | solution.py:96
  311.4 3.2 fusion.292
  314.6 1.2 maximum_convert_fusion.3
  316.3 8.4 %fusion.486 = f32[256,1024]{1,0:T(8,128)} fusion(f32[383,1024]{1,0:T(8,128)S(1)} %maximum_convert_fusion.3, f32[256]{0:T(256)} %get-tuple-element.407, f32[256]{0:T(256)} %get-tuple-element.408, f32[256]{0:T(256)} %get-tuple-element.409, f32[256]{0:T(256)} %get-tuple-element.410, f32[256]{0:T(256)} %get-tuple-element.411, f32[256]{0:T(256)} %get-tuple-element.412, ...), kind=kLoop, calls=%fused_computation.732 | loop fusion | flops 24903680 | bytes 34766848 | tf_op jit(solution)/shard_map/add | solution.py:43
  324.8 25.0 %fusion.548 = (bf16[256,1,1024]{2,0,1:T(8,128)(2,1)}, f32[256,1024]{1,0:T(8,128)}) fusion(f32[256,3,1024]{2,0,1:T(8,128)} %copy-done.4, f32[256]{0:T(256)} %get-tuple-element.307, f32[383,1024]{1,0:T(8,128)S(1)} %maximum_convert_fusion.3, f32[1024]{0:T(1024)S(1)} %bitcast.280, f32[256]{0:T(256)} %get-tuple-element.308, f32[1024]{0:T(1024)S(1)} %bitcast.282, ...), kind=kLoop, calls=%fused_computation.838 | loop fusion | flops 76021760 | bytes 104824832 | tf_op jit(solution)/shard_map/stack | solution.py:96
  349.9 3.4 fusion.549
  353.9 1.3 collective-permute-start.3
  416.0 10.6 %stack.704 = bf16[128,1024]{1,0:T(8,128)(2,1)} concatenate(bf16[1,1024]{1,0:T(2,128)(2,1)S(1)} %stack.576, bf16[1,1024]{1,0:T(2,128)(2,1)S(1)} %stack.577, bf16[1,1024]{1,0:T(2,128)(2,1)S(1)} %stack.578, bf16[1,1024]{1,0:T(2,128)(2,1)S(1)} %stack.579, bf16[1,1024]{1,0:T(2,128)(2,1)S(1)} %stack.580, bf16[1,1024]{1,0:T(2,128)(2,1)S(1)} %stack.581, bf16[1,1024]{1,0:T(2,128)(2,1)S(1)} %stack.582, ...), dimensions={0} | concatenate | bytes 524288 | tf_op jit(solution)/shard_map/stack | solution.py:55
  427.2 3.9 fusion.17
  431.0 13.2 %fusion = bf16[256,4096]{1,0:T(8,128)(2,1)} fusion(bf16[256,3,1024]{2,0,1:T(8,128)(2,1)S(1)} %fusion.17, bf16[4096,3,1024]{2,0,1:T(8,128)(2,1)} %all-gather.5.cloned.1.call-done), kind=kOutput, calls=%fused_computation.137 | convolution fusion | flops 6443499520 | bytes 28835840 | tf_op jit(solution)/shard_map/tsc,dsc->td/dot_general | solution.py:127
  444.3 13.5 %convolution_convert_fusion = bf16[4096,3,1024]{2,0,1:T(8,128)(2,1)} fusion(bf16[256,3,1024]{2,0,1:T(8,128)(2,1)S(1)} %fusion.17, bf16[256,4096]{1,0:T(8,128)(2,1)} %all-gather.3.cloned.1.call-done), kind=kOutput, calls=%fused_computation.128 | convolution fusion | flops 6455033856 | bytes 28835840 | tf_op jit(solution)/shard_map/td,tsc->dsc/dot_general | solution.py:134
  457.8 31.4 %all-reduce.2.cloned.1.call-done = bf16[128,1024]{1,0:T(8,128)(2,1)} async-done(((bf16[128,1024]{1,0:T(8,128)(2,1)}), bf16[128,1024]{1,0:T(8,128)(2,1)}) %all-reduce.2.cloned.1.call-update) | async-done | bytes 262160 | tf_op jit(solution)/shard_map/psum | solution.py:125
  489.2 1.9 convert_element_type.1809
  491.1 2.1 fusion.2
  493.3 3.7 fusion.14
  497.1 23.5 %psum.14 = bf16[3,7,1024]{2,0,1:T(4,128)(2,1)S(1)} all-reduce(bf16[3,7,1024]{2,0,1:T(4,128)(2,1)S(1)} %bitcast.214), channel_id=1, replica_groups=mesh['ctx'=8,'fsdp'=4] {'ctx'}, use_global_device_ids=true, to_apply=%region_13.14 | all-reduce | flops 21504 | bytes 86016 | tf_op jit(solution)/shard_map/psum | solution.py:122
  521.3 14.0 %reduce-scatter.3.cloned.1.call-done = bf16[256,1024]{1,0:T(8,128)(2,1)} async-done(((bf16[256,4096]{1,0:T(8,128)(2,1)}), bf16[256,1024]{1,0:T(8,128)(2,1)}) %reduce-scatter.3.cloned.1.call-update) | async-done | bytes 524304 | tf_op jit(solution)/shard_map/reduce_scatter | solution.py:130
  535.3 160.2 %reduce-scatter.5.cloned.1.call-done = bf16[512,3,1024]{2,0,1:T(8,128)(2,1)} async-done(((bf16[4096,3,1024]{2,0,1:T(8,128)(2,1)}), bf16[512,3,1024]{2,0,1:T(8,128)(2,1)}) %reduce-scatter.5.cloned.1.call-update) | async-done | bytes 3145744 | tf_op jit(solution)/shard_map/reduce_scatter | solution.py:133
  (555 shorter events, 72.3 us)
Async XLA Ops:
  7.2 78.8 %all-gather.3.cloned.1.call-start = ((), (), s32[]{:S(2)}) async-start(), calls=%async_computation.3 | async-start | bytes 2621440 | tf_op jit(solution)/shard_map/all_gather | solution.py:70
  40.6 171.5 %all-gather.5.cloned.1.call-start = ((), (), s32[]{:S(2)}) async-start(), calls=%async_computation.4 | async-start | bytes 28311552 | tf_op jit(solution)/shard_map/all_gather | solution.py:71
  41.3 447.9 %all-reduce.2.cloned.1.call-start = ((), (), s32[]{:S(2)}) async-start(), calls=%async_computation.7 | async-start | bytes 524288 | tf_op jit(solution)/shard_map/psum | solution.py:125
  52.7 175.1 %copy-start.89 = (f32[256]{0:T(256)}, f32[256]{0:T(256)S(1)}, u32[]{:S(2)}) copy-start(f32[256]{0:T(256)S(1)} %get-tuple-element.555) | copy-start | bytes 3076
  52.7 175.1 %copy-start.92 = (f32[256]{0:T(256)}, f32[256]{0:T(256)S(1)}, u32[]{:S(2)}) copy-start(f32[256]{0:T(256)S(1)} %get-tuple-element.556) | copy-start | bytes 3076
  52.7 175.1 %copy-start.95 = (f32[256]{0:T(256)}, f32[256]{0:T(256)S(1)}, u32[]{:S(2)}) copy-start(f32[256]{0:T(256)S(1)} %get-tuple-element.557) | copy-start | bytes 3076
  52.7 175.1 %copy-start.98 = (f32[256]{0:T(256)}, f32[256]{0:T(256)S(1)}, u32[]{:S(2)}) copy-start(f32[256]{0:T(256)S(1)} %get-tuple-element.558) | copy-start | bytes 3076
  52.7 175.1 %copy-start.101 = (f32[256]{0:T(256)}, f32[256]{0:T(256)S(1)}, u32[]{:S(2)}) copy-start(f32[256]{0:T(256)S(1)} %get-tuple-element.559) | copy-start | bytes 3076
  52.7 175.1 %copy-start.104 = (f32[256]{0:T(256)}, f32[256]{0:T(256)S(1)}, u32[]{:S(2)}) copy-start(f32[256]{0:T(256)S(1)} %get-tuple-element.560) | copy-start | bytes 3076
  52.7 175.1 %copy-start.106 = (f32[256]{0:T(256)}, f32[256]{0:T(256)S(1)}, u32[]{:S(2)}) copy-start(f32[256]{0:T(256)S(1)} %get-tuple-element.561) | copy-start | bytes 3076
  52.7 184.2 %copy-start.138 = (f32[256]{0:T(256)}, f32[256]{0:T(256)S(1)}, u32[]{:S(2)}) copy-start(f32[256]{0:T(256)S(1)} %get-tuple-element.448) | copy-start | bytes 3076
  52.7 212.7 %copy-start.108 = (f32[256]{0:T(256)}, f32[256]{0:T(256)S(1)}, u32[]{:S(2)}) copy-start(f32[256]{0:T(256)S(1)} %get-tuple-element.519) | copy-start | bytes 3076
  52.7 212.7 %copy-start.109 = (f32[256]{0:T(256)}, f32[256]{0:T(256)S(1)}, u32[]{:S(2)}) copy-start(f32[256]{0:T(256)S(1)} %get-tuple-element.520) | copy-start | bytes 3076
  52.8 216.0 %copy-start.110 = (f32[256]{0:T(256)}, f32[256]{0:T(256)S(1)}, u32[]{:S(2)}) copy-start(f32[256]{0:T(256)S(1)} %get-tuple-element.521) | copy-start | bytes 3076
  52.8 215.9 %copy-start.111 = (f32[256]{0:T(256)}, f32[256]{0:T(256)S(1)}, u32[]{:S(2)}) copy-start(f32[256]{0:T(256)S(1)} %get-tuple-element.522) | copy-start | bytes 3076
  52.8 215.9 %copy-start.112 = (f32[256]{0:T(256)}, f32[256]{0:T(256)S(1)}, u32[]{:S(2)}) copy-start(f32[256]{0:T(256)S(1)} %get-tuple-element.523) | copy-start | bytes 3076
  52.8 215.9 %copy-start.113 = (f32[256]{0:T(256)}, f32[256]{0:T(256)S(1)}, u32[]{:S(2)}) copy-start(f32[256]{0:T(256)S(1)} %get-tuple-element.524) | copy-start | bytes 3076
  52.8 215.9 %copy-start.114 = (f32[256]{0:T(256)}, f32[256]{0:T(256)S(1)}, u32[]{:S(2)}) copy-start(f32[256]{0:T(256)S(1)} %get-tuple-element.525) | copy-start | bytes 3076
  52.8 215.9 %copy-start.115 = (f32[256]{0:T(256)}, f32[256]{0:T(256)S(1)}, u32[]{:S(2)}) copy-start(f32[256]{0:T(256)S(1)} %get-tuple-element.526) | copy-start | bytes 3076
  52.8 215.9 %copy-start.116 = (f32[256]{0:T(256)}, f32[256]{0:T(256)S(1)}, u32[]{:S(2)}) copy-start(f32[256]{0:T(256)S(1)} %get-tuple-element.527) | copy-start | bytes 3076
  52.8 215.9 %copy-start.117 = (f32[256]{0:T(256)}, f32[256]{0:T(256)S(1)}, u32[]{:S(2)}) copy-start(f32[256]{0:T(256)S(1)} %get-tuple-element.528) | copy-start | bytes 3076
  52.8 219.2 %copy-start.118 = (f32[256]{0:T(256)}, f32[256]{0:T(256)S(1)}, u32[]{:S(2)}) copy-start(f32[256]{0:T(256)S(1)} %get-tuple-element.529) | copy-start | bytes 3076
  52.8 219.2 %copy-start.119 = (f32[256]{0:T(256)}, f32[256]{0:T(256)S(1)}, u32[]{:S(2)}) copy-start(f32[256]{0:T(256)S(1)} %get-tuple-element.530) | copy-start | bytes 3076
  52.9 219.2 %copy-start.120 = (f32[256]{0:T(256)}, f32[256]{0:T(256)S(1)}, u32[]{:S(2)}) copy-start(f32[256]{0:T(256)S(1)} %get-tuple-element.531) | copy-start | bytes 3076
  52.9 219.2 %copy-start.121 = (f32[256]{0:T(256)}, f32[256]{0:T(256)S(1)}, u32[]{:S(2)}) copy-start(f32[256]{0:T(256)S(1)} %get-tuple-element.532) | copy-start | bytes 3076
  52.9 219.2 %copy-start.122 = (f32[256]{0:T(256)}, f32[256]{0:T(256)S(1)}, u32[]{:S(2)}) copy-start(f32[256]{0:T(256)S(1)} %get-tuple-element.533) | copy-start | bytes 3076
  52.9 219.2 %copy-start.123 = (f32[256]{0:T(256)}, f32[256]{0:T(256)S(1)}, u32[]{:S(2)}) copy-start(f32[256]{0:T(256)S(1)} %get-tuple-element.534) | copy-start | bytes 3076
  52.9 219.2 %copy-start.124 = (f32[256]{0:T(256)}, f32[256]{0:T(256)S(1)}, u32[]{:S(2)}) copy-start(f32[256]{0:T(256)S(1)} %get-tuple-element.535) | copy-start | bytes 3076
  52.9 219.2 %copy-start.125 = (f32[256]{0:T(256)}, f32[256]{0:T(256)S(1)}, u32[]{:S(2)}) copy-start(f32[256]{0:T(256)S(1)} %get-tuple-element.536) | copy-start | bytes 3076
  52.9 222.5 %copy-start.126 = (f32[256]{0:T(256)}, f32[256]{0:T(256)S(1)}, u32[]{:S(2)}) copy-start(f32[256]{0:T(256)S(1)} %get-tuple-element.537) | copy-start | bytes 3076
  52.9 222.5 %copy-start.127 = (f32[256]{0:T(256)}, f32[256]{0:T(256)S(1)}, u32[]{:S(2)}) copy-start(f32[256]{0:T(256)S(1)} %get-tuple-element.538) | copy-start | bytes 3076
  52.9 222.5 %copy-start.128 = (f32[256]{0:T(256)}, f32[256]{0:T(256)S(1)}, u32[]{:S(2)}) copy-start(f32[256]{0:T(256)S(1)} %get-tuple-element.539) | copy-start | bytes 3076
  52.9 222.5 %copy-start.129 = (f32[256]{0:T(256)}, f32[256]{0:T(256)S(1)}, u32[]{:S(2)}) copy-start(f32[256]{0:T(256)S(1)} %get-tuple-element.540) | copy-start | bytes 3076
  53.0 222.5 %copy-start.130 = (f32[256]{0:T(256)}, f32[256]{0:T(256)S(1)}, u32[]{:S(2)}) copy-start(f32[256]{0:T(256)S(1)} %get-tuple-element.541) | copy-start | bytes 3076
  53.0 222.5 %copy-start.131 = (f32[256]{0:T(256)}, f32[256]{0:T(256)S(1)}, u32[]{:S(2)}) copy-start(f32[256]{0:T(256)S(1)} %get-tuple-element.542) | copy-start | bytes 3076
  53.0 222.5 %copy-start.132 = (f32[256]{0:T(256)}, f32[256]{0:T(256)S(1)}, u32[]{:S(2)}) copy-start(f32[256]{0:T(256)S(1)} %get-tuple-element.543) | copy-start | bytes 3076
  53.0 222.5 %copy-start.133 = (f32[256]{0:T(256)}, f32[256]{0:T(256)S(1)}, u32[]{:S(2)}) copy-start(f32[256]{0:T(256)S(1)} %get-tuple-element.544) | copy-start | bytes 3076
  53.0 225.9 %copy-start.134 = (f32[256]{0:T(256)}, f32[256]{0:T(256)S(1)}, u32[]{:S(2)}) copy-start(f32[256]{0:T(256)S(1)} %get-tuple-element.545) | copy-start | bytes 3076
  53.0 225.9 %copy-start.135 = (f32[256]{0:T(256)}, f32[256]{0:T(256)S(1)}, u32[]{:S(2)}) copy-start(f32[256]{0:T(256)S(1)} %get-tuple-element.546) | copy-start | bytes 3076
  53.0 225.9 %copy-start.136 = (f32[256]{0:T(256)}, f32[256]{0:T(256)S(1)}, u32[]{:S(2)}) copy-start(f32[256]{0:T(256)S(1)} %get-tuple-element.547) | copy-start | bytes 3076
  224.2 3.0 collective-permute-start
  231.7 5.0 collective-permute-start.1
  240.4 70.8 %copy-start.2 = (bf16[256,1024]{1,0:T(8,128)(2,1)}, bf16[256,1024]{1,0:T(8,128)(2,1)S(1)}, u32[]{:S(2)}) copy-start(bf16[256,1024]{1,0:T(8,128)(2,1)S(1)} %get-tuple-element.154) | copy-start | bytes 1572868
  241.2 73.5 %collective-permute-start.2 = (bf16[127,1024]{1,0:T(8,128)(2,1)}, bf16[127,1024]{1,0:T(8,128)(2,1)S(1)}, u32[]{:S(2)}, u32[]{:S(2)}) collective-permute-start(bf16[127,1024]{1,0:T(8,128)(2,1)} %slice.2608), channel_id=1, source_target_pairs={{4,0},{8,4},{12,8},{16,12},{20,16},{24,20},{28,24},{5,1},{9,5},{13... | collective-permute-start | bytes 780296 | tf_op jit(solution)/shard_map/ppermute | solution.py:10
  353.3 73.4 %copy-start.9 = (bf16[256,1,1024]{2,0,1:T(8,128)(2,1)}, bf16[256,1,1024]{2,0,1:T(8,128)(2,1)S(1)}, u32[]{:S(2)}) copy-start(bf16[256,1,1024]{2,0,1:T(8,128)(2,1)S(1)} %get-tuple-element.162) | copy-start | bytes 1572868
  353.9 72.8 %collective-permute-start.3 = (bf16[6,3,1024]{2,0,1:T(8,128)(2,1)S(1)}, bf16[6,3,1024]{2,0,1:T(8,128)(2,1)S(1)}, u32[]{:S(2)}, u32[]{:S(2)}) collective-permute-start(bf16[6,3,1024]{2,0,1:T(8,128)(2,1)S(1)} %slice.2737), channel_id=1, source_target_pairs={{4,0},{8,4},{12,8},{16,12},{20,16},{24,20},{28,24},{5,1},{9,5},{13... | collective-permute-start | bytes 110600 | tf_op jit(solution)/shard_map/ppermute | solution.py:10
  426.6 108.7 %reduce-scatter.3.cloned.1.call-start = ((), (), s32[]{:S(2)}) async-start(), calls=%async_computation.5 | async-start | bytes 2621440 | tf_op jit(solution)/shard_map/reduce_scatter | solution.py:130
  444.2 251.3 %reduce-scatter.5.cloned.1.call-start = ((), (), s32[]{:S(2)}) async-start(), calls=%async_computation.6 | async-start | bytes 28311552 | tf_op jit(solution)/shard_map/reduce_scatter | solution.py:133
  (146 other events, 2949.4 us)
Sparse Core Ops, SparseCore 0:
  40.7 45.3 all-gather.2
  87.9 124.0 all-gather.4
  426.8 62.3 all-reduce.1
  492.0 43.2 reduce-scatter.2
  539.4 156.1 reduce-scatter.4
where the time goes:
time: 712 us; the launch traced here: 702 us
  waiting for transfers between devices  366 us (51%)
  other arithmetic  137 us (19%)
  local copies, waits for them, and re-layouts  77.5 us (11%)
  blocking collectives  55.3 us (8%)
  matrix products  40.3 us (6%)
  between operations  17.3 us (2%)
  starting transfers between devices  8.79 us (1%)
    reduce_scatter x1, waiting for transfers between devices, on_device(): lax.psum_scatter(jnp.einsum('td,tsc->dsc', tokens, grad_mixed, preferred_...  160 us
    all_gather x1, waiting for transfers between devices, on_device(): gathered = lax.all_gather(w_in, 'ctx', axis=0, tiled=True)  126 us
    another operation x130, local copies, waits for them, and re-layouts, tap_sums(): return jnp.stack(pieces, 0)  70.2 us
    reduce_sum x17, other arithmetic, tap_sums(): pieces.append(jnp.sum(grads * ext[first:first + count] * keep_mask, axis=0))  52.3 us
    another operation x4, other arithmetic, on_device(): jnp.stack([first_grad, grad_product * filtered[:, 2], grad_product * filt...  47.6 us
    all_gather x1, waiting for transfers between devices, on_device(): tokens = lax.all_gather(own_part, 'fsdp', axis=1, tiled=True)  33 us
    all_to_all x1, blocking collectives, on_device(): lax.all_to_all(loaded, 'ctx', split_axis=1, concat_axis=0, tiled=True)  31.8 us
    psum x1, waiting for transfers between devices, on_device(): lax.psum(long_local.astype(jnp.bfloat16), 'ctx').astype(jnp.float32)  31.4 us
  transfers between devices with their start and end apart: 9, of which 6 were waited for; matrix products, arithmetic and copies ran while one was open for 28% of the time, Pallas kernels for 0%

commit v1 on v0

--- a/solution.py
+++ b/solution.py
@@ -1,7 +1,24 @@
+import functools
 import jax
 import jax.numpy as jnp
 from jax import lax
 from jax.sharding import PartitionSpec as P
+
+
+def _use_panels(mine, ndim_at):
+    nodes = lax.psum(1, axis_name="fsdp")
+    ready = mine
+    gallery = [ready]
+    arr_out = sorted(((d, (d + 1) % nodes) for d in range(nodes)))
+    for dd in tuple(range(1, nodes)):
+        ready = lax.ppermute(ready, perm=arr_out, axis_name="fsdp")
+        gallery.insert(0, ready)
+    value_now = jnp.concatenate(gallery, axis=ndim_at)
+    high = lax.axis_index("fsdp") + 1
+    return jnp.roll(value_now, high * mine.shape[ndim_at], axis=ndim_at)
+
+
+group_the_records = functools.partial(_use_panels, ndim_at=1)
 
 
 def passed_along(x, axis, by):
@@ -67,7 +84,7 @@
         jnp.bfloat16
     )
     own_part = jnp.dot(picker, slot_rows, preferred_element_type=jnp.float32).astype(jnp.bfloat16)
-    tokens = lax.all_gather(own_part, "fsdp", axis=1, tiled=True)
+    tokens = group_the_records(own_part)
     gathered = lax.all_gather(w_in, "ctx", axis=0, tiled=True)
     streams = jnp.einsum("td,dsc->tsc", tokens, gathered, preferred_element_type=jnp.float32)
     proj_half = streams.astype(jnp.bfloat16)

time: 712 us -> 651 us (0.914)
  waiting for transfers between devices: 366 us -> 322 us
  blocking collectives: 55.3 us -> 23.7 us
  starting transfers between devices: 8.79 us -> 17.1 us
    all_gather x1, waiting for transfers between devices: 126 us -> 54.6 us  [on_device(): gathered = lax.all_gather(w_in, 'ctx', axis=0, tiled=True)]
    all_to_all x0 -> x1, waiting for transfers between devices: none -> 34 us  [on_device(): lax.all_to_all(loaded, 'ctx', split_axis=1, concat_axis=0, tiled=True)]
    all_gather x1 -> x0, waiting for transfers between devices: 33 us -> none  [on_device(): tokens = lax.all_gather(own_part, 'fsdp', axis=1, tiled=True)]
    all_to_all x1 -> x0, blocking collectives: 31.8 us -> none  [on_device(): lax.all_to_all(loaded, 'ctx', split_axis=1, concat_axis=0, tiled=True)]
    ppermute x0 -> x3, waiting for transfers between devices: none -> 26.8 us  [_use_panels(): ready = lax.ppermute(ready, perm=arr_out, axis_name='fsdp')]
  transfers between devices with their start and end apart: 9 -> 12, of which waited for: 6 -> 9; matrix products, arithmetic and copies ran while one was open for 28% -> 31% of each run, Pallas kernels for 0% -> 0%
where the time goes in v1:
time: 651 us; the launch traced here: 641 us
  waiting for transfers between devices  322 us (49%)
  other arithmetic  138 us (21%)
  local copies, waits for them, and re-layouts  84.1 us (13%)
  matrix products  39.5 us (6%)
  blocking collectives  23.7 us (4%)
  between operations  17.3 us (3%)
  starting transfers between devices  17.1 us (3%)
    reduce_scatter x1, waiting for transfers between devices, on_device(): lax.psum_scatter(jnp.einsum('td,tsc->dsc', tokens, grad_mixed, preferred_...  160 us
    another operation x130, local copies, waits for them, and re-layouts, tap_sums(): return jnp.stack(pieces, 0)  69.7 us
    all_gather x1, waiting for transfers between devices, on_device(): gathered = lax.all_gather(w_in, 'ctx', axis=0, tiled=True)  54.6 us
    reduce_sum x17, other arithmetic, tap_sums(): pieces.append(jnp.sum(grads * ext[first:first + count] * keep_mask, axis=0))  52.4 us
    another operation x4, other arithmetic, on_device(): jnp.stack([first_grad, grad_product * filtered[:, 2], grad_product * filt...  47.7 us
    all_to_all x1, waiting for transfers between devices, on_device(): lax.all_to_all(loaded, 'ctx', split_axis=1, concat_axis=0, tiled=True)  34 us
    psum x1, waiting for transfers between devices, on_device(): lax.psum(long_local.astype(jnp.bfloat16), 'ctx').astype(jnp.float32)  31.4 us
    ppermute x3, waiting for transfers between devices, _use_panels(): ready = lax.ppermute(ready, perm=arr_out, axis_name='fsdp')  26.8 us
  transfers between devices with their start and end apart: 12, of which 9 were waited for; matrix products, arithmetic and copies ran while one was open for 31% of the time, Pallas kernels for 0%

profile of v1, /device:TPU:0, one launch (start us, length us, event | category | flops | bytes accessed | tf_op | source)
XLA Modules:
  0.0 641.2 jit_solution(2201271811482145461)
XLA Ops:
  7.9 5.3 all-to-all-start
  19.6 34.0 %all-to-all-done = bf16[1,8,128,1024]{3,2,0,1:T(8,128)(2,1)S(1)} async-done(((bf16[1,8,128,1024]{3,2,0,1:T(8,128)(2,1)}), bf16[1,8,128,1024]{3,2,0,1:T(8,128)(2,1)S(1)}, u32[]{:S(2)}, u32[]{:S(2)}) %all-to-all-start) | async-done | bytes 2097184 | tf_op jit(solution)/shard_map/all_to_all | solution.py:76
  54.4 1.7 collective-permute-start
  57.5 9.0 %collective-permute-done = bf16[256,1024]{1,0:T(8,128)(2,1)S(1)} collective-permute-done((bf16[256,1024]{1,0:T(8,128)(2,1)S(1)}, bf16[256,1024]{1,0:T(8,128)(2,1)S(1)}, u32[]{:S(2)}, u32[]{:S(2)}) %collective-permute-start) | collective-permute-done | bytes 524320 | tf_op jit(solution)/shard_map/ppermute | solution.py:14
  68.6 10.0 %collective-permute-done.1 = bf16[256,1024]{1,0:T(8,128)(2,1)S(1)} collective-permute-done((bf16[256,1024]{1,0:T(8,128)(2,1)S(1)}, bf16[256,1024]{1,0:T(8,128)(2,1)S(1)}, u32[]{:S(2)}, u32[]{:S(2)}) %collective-permute-start.1) | collective-permute-done | bytes 524320 | tf_op jit(solution)/shard_map/ppermute | solution.py:14
  80.0 1.4 compare_convert_fusion.219
  81.8 7.8 %collective-permute-done.2 = bf16[256,1024]{1,0:T(8,128)(2,1)S(1)} collective-permute-done((bf16[256,1024]{1,0:T(8,128)(2,1)S(1)}, bf16[256,1024]{1,0:T(8,128)(2,1)S(1)}, u32[]{:S(2)}, u32[]{:S(2)}) %collective-permute-start.2) | collective-permute-done | bytes 524320 | tf_op jit(solution)/shard_map/ppermute | solution.py:14
  89.6 0.9 constant_dynamic-update-slice_fusion.7
  91.4 0.9 constant_dynamic-update-slice_fusion.5
  94.0 0.9 constant_dynamic-update-slice_fusion.2
  96.6 54.6 %all-gather.2.cloned.1.call-done = bf16[4096,3,1024]{2,0,1:T(8,128)(2,1)} async-done(((bf16[512,3,1024]{2,0,1:T(8,128)(2,1)}), bf16[4096,3,1024]{2,0,1:T(8,128)(2,1)}) %all-gather.2.cloned.1.call-update) | async-done | bytes 25165840 | tf_op jit(solution)/shard_map/all_gather | solution.py:88
  151.2 12.2 %fusion.34 = bf16[256,3,1024]{2,0,1:T(8,128)(2,1)S(1)} fusion(bf16[4096,3,1024]{2,0,1:T(8,128)(2,1)} %all-gather.2.cloned.1.call-done, bf16[256,8192]{1,0:T(8,128)(2,1)} %constant_dynamic-update-slice_fusion, s32[]{:T(128)S(6)} %select_n.26), kind=kOutput, calls=%fused_computation.179 | convolution fusion | flops 6443237376 | bytes 28835844 | tf_op jit(solution)/shard_map/td,dsc->tsc/dot_general | solution.py:89
  163.4 2.2 collective-permute-start.3
  167.0 3.6 multiply_add_fusion
  170.9 3.7 collective-permute-start.4
  176.1 3.4 fusion.268
  180.3 1.5 collective-permute-start.5
  181.8 3.3 fusion.270
  185.1 3.3 fusion.272
  188.4 3.3 fusion.274
  191.7 3.3 fusion.276
  195.0 3.1 fusion.278
  198.1 3.3 fusion.280
  201.4 3.3 fusion.282
  204.6 3.3 fusion.284
  208.0 3.3 fusion.286
  211.3 3.3 fusion.288
  214.7 3.5 fusion.290
  218.6 3.3 fusion.292
  222.3 9.1 %multiply_add_fusion.2 = f32[256,1024]{1,0:T(8,128)S(1)} fusion(f32[383,1024]{1,0:T(8,128)S(1)} %maximum_convert_fusion.2, f32[256]{0:T(256)} %copy-done.108, f32[1024]{0:T(1024)S(1)} %bitcast.308, f32[256]{0:T(256)} %copy-done.109, f32[1024]{0:T(1024)S(1)} %bitcast.311, f32[256]{0:T(256)} %copy-done.110, f32[1024]{0:T(1024)S(1)} %bitcast.313, ...), kind=kLoop, calls=%fused_computation.834 | loop fusion | flops 33554432 | bytes 46357504 | tf_op jit(solution)/shard_map/add | solution.py:45
  231.4 19.1 %fusion.552 = (bf16[256,1,1024]{2,0,1:T(8,128)(2,1)}, f32[256,1024]{1,0:T(8,128)}) fusion(bf16[256,1024]{1,0:T(8,128)(2,1)} %param.13, f32[256]{0:T(256)} %get-tuple-element.435, f32[383,1024]{1,0:T(8,128)S(1)} %maximum_convert_fusion.2, f32[1024]{0:T(1024)} %bitcast.278, f32[256]{0:T(256)} %get-tuple-element.436, f32[1024]{0:T(1024)} %bitcast.280, ...), kind=kLoop, calls=%fused_computation.842 | loop fusion | flops 67633152 | bytes 92709888 | tf_op jit(solution)/shard_map/stack | solution.py:113
  250.7 3.2 fusion.294
  253.9 1.2 maximum_convert_fusion.3
  255.5 8.4 %fusion.488 = f32[256,1024]{1,0:T(8,128)} fusion(f32[383,1024]{1,0:T(8,128)S(1)} %maximum_convert_fusion.3, f32[256]{0:T(256)} %get-tuple-element.407, f32[256]{0:T(256)} %get-tuple-element.408, f32[256]{0:T(256)} %get-tuple-element.409, f32[256]{0:T(256)} %get-tuple-element.410, f32[256]{0:T(256)} %get-tuple-element.411, f32[256]{0:T(256)} %get-tuple-element.412, ...), kind=kLoop, calls=%fused_computation.734 | loop fusion | flops 24903680 | bytes 34766848 | tf_op jit(solution)/shard_map/add | solution.py:60
  264.1 25.0 %fusion.550 = (bf16[256,1,1024]{2,0,1:T(8,128)(2,1)}, f32[256,1024]{1,0:T(8,128)}) fusion(f32[256,3,1024]{2,0,1:T(8,128)} %copy-done.4, f32[256]{0:T(256)} %get-tuple-element.307, f32[383,1024]{1,0:T(8,128)S(1)} %maximum_convert_fusion.3, f32[1024]{0:T(1024)S(1)} %bitcast.279, f32[256]{0:T(256)} %get-tuple-element.308, f32[1024]{0:T(1024)S(1)} %bitcast.281, ...), kind=kLoop, calls=%fused_computation.840 | loop fusion | flops 76021760 | bytes 104824832 | tf_op jit(solution)/shard_map/stack | solution.py:113
  289.1 3.4 fusion.551
  293.1 1.3 collective-permute-start.6
  354.7 10.6 %stack.704 = bf16[128,1024]{1,0:T(8,128)(2,1)} concatenate(bf16[1,1024]{1,0:T(2,128)(2,1)S(1)} %stack.576, bf16[1,1024]{1,0:T(2,128)(2,1)S(1)} %stack.577, bf16[1,1024]{1,0:T(2,128)(2,1)S(1)} %stack.578, bf16[1,1024]{1,0:T(2,128)(2,1)S(1)} %stack.579, bf16[1,1024]{1,0:T(2,128)(2,1)S(1)} %stack.580, bf16[1,1024]{1,0:T(2,128)(2,1)S(1)} %stack.581, bf16[1,1024]{1,0:T(2,128)(2,1)S(1)} %stack.582, ...), dimensions={0} | concatenate | bytes 524288 | tf_op jit(solution)/shard_map/stack | solution.py:72
  365.9 3.9 fusion.17
  369.8 13.2 %fusion = bf16[256,4096]{1,0:T(8,128)(2,1)} fusion(bf16[256,3,1024]{2,0,1:T(8,128)(2,1)S(1)} %fusion.17, bf16[4096,3,1024]{2,0,1:T(8,128)(2,1)} %all-gather.2.cloned.1.call-done), kind=kOutput, calls=%fused_computation.137 | convolution fusion | flops 6443499520 | bytes 28835840 | tf_op jit(solution)/shard_map/tsc,dsc->td/dot_general | solution.py:144
  383.0 13.5 %convolution_convert_fusion = bf16[4096,3,1024]{2,0,1:T(8,128)(2,1)} fusion(bf16[256,3,1024]{2,0,1:T(8,128)(2,1)S(1)} %fusion.17, bf16[256,8192]{1,0:T(8,128)(2,1)} %constant_dynamic-update-slice_fusion, s32[]{:T(128)S(6)} %select_n.26), kind=kOutput, calls=%fused_computation.128 | convolution fusion | flops 6455033856 | bytes 28835844 | tf_op jit(solution)/shard_map/td,tsc->dsc/dot_general | solution.py:151
  396.6 31.4 %all-reduce.2.cloned.1.call-done = bf16[128,1024]{1,0:T(8,128)(2,1)} async-done(((bf16[128,1024]{1,0:T(8,128)(2,1)}), bf16[128,1024]{1,0:T(8,128)(2,1)}) %all-reduce.2.cloned.1.call-update) | async-done | bytes 262160 | tf_op jit(solution)/shard_map/psum | solution.py:142
  427.9 1.9 convert_element_type.1809
  429.9 2.1 fusion.2
  432.0 3.7 fusion.14
  435.9 23.7 %psum.14 = bf16[3,7,1024]{2,0,1:T(4,128)(2,1)S(1)} all-reduce(bf16[3,7,1024]{2,0,1:T(4,128)(2,1)S(1)} %bitcast.213), channel_id=1, replica_groups=mesh['ctx'=8,'fsdp'=4] {'ctx'}, use_global_device_ids=true, to_apply=%region_13.14 | all-reduce | flops 21504 | bytes 86016 | tf_op jit(solution)/shard_map/psum | solution.py:139
  460.2 14.0 %reduce-scatter.3.cloned.1.call-done = bf16[256,1024]{1,0:T(8,128)(2,1)} async-done(((bf16[256,4096]{1,0:T(8,128)(2,1)}), bf16[256,1024]{1,0:T(8,128)(2,1)}) %reduce-scatter.3.cloned.1.call-update) | async-done | bytes 524304 | tf_op jit(solution)/shard_map/reduce_scatter | solution.py:147
  474.2 160.3 %reduce-scatter.5.cloned.1.call-done = bf16[512,3,1024]{2,0,1:T(8,128)(2,1)} async-done(((bf16[4096,3,1024]{2,0,1:T(8,128)(2,1)}), bf16[512,3,1024]{2,0,1:T(8,128)(2,1)}) %reduce-scatter.5.cloned.1.call-update) | async-done | bytes 3145744 | tf_op jit(solution)/shard_map/reduce_scatter | solution.py:150
  (567 shorter events, 82.5 us)
Async XLA Ops:
  7.2 144.0 %all-gather.2.cloned.1.call-start = ((), (), s32[]{:S(2)}) async-start(), calls=%async_computation.3 | async-start | bytes 28311552 | tf_op jit(solution)/shard_map/all_gather | solution.py:88
  7.9 45.7 %all-to-all-start = ((bf16[1,8,128,1024]{3,2,0,1:T(8,128)(2,1)}), bf16[1,8,128,1024]{3,2,0,1:T(8,128)(2,1)S(1)}, u32[]{:S(2)}, u32[]{:S(2)}) async-start(bf16[1,8,128,1024]{3,2,0,1:T(8,128)(2,1)} %bitcast.2), calls=%async_computation | async-start | bytes 4194304 | tf_op jit(solution)/shard_map/all_to_all | solution.py:76
  13.3 414.7 %all-reduce.2.cloned.1.call-start = ((), (), s32[]{:S(2)}) async-start(), calls=%async_computation.6 | async-start | bytes 524288 | tf_op jit(solution)/shard_map/psum | solution.py:142
  54.4 12.2 %collective-permute-start = (bf16[256,1024]{1,0:T(8,128)(2,1)S(1)}, bf16[256,1024]{1,0:T(8,128)(2,1)S(1)}, u32[]{:S(2)}, u32[]{:S(2)}) collective-permute-start(bf16[256,1024]{1,0:T(8,128)(2,1)S(1)} %convolution_convert_fusion.1), channel_id=1, source_target_pairs={{0,1},{1,2},{2,3},{3,0},{4,5},{5,6},{6,7},{7,4},{8,9},{9,10},{10,1... | collective-permute-start | bytes 1572872 | tf_op jit(solution)/shard_map/ppermute | solution.py:14
  66.5 12.1 %collective-permute-start.1 = (bf16[256,1024]{1,0:T(8,128)(2,1)S(1)}, bf16[256,1024]{1,0:T(8,128)(2,1)S(1)}, u32[]{:S(2)}, u32[]{:S(2)}) collective-permute-start(bf16[256,1024]{1,0:T(8,128)(2,1)S(1)} %collective-permute-done), channel_id=1, source_target_pairs={{0,1},{1,2},{2,3},{3,0},{4,5},{5,6},{6,7},{7,4},{8,9},{9,10},{10,1... | collective-permute-start | bytes 1572872 | tf_op jit(solution)/shard_map/ppermute | solution.py:14
  78.6 11.0 %collective-permute-start.2 = (bf16[256,1024]{1,0:T(8,128)(2,1)S(1)}, bf16[256,1024]{1,0:T(8,128)(2,1)S(1)}, u32[]{:S(2)}, u32[]{:S(2)}) collective-permute-start(bf16[256,1024]{1,0:T(8,128)(2,1)S(1)} %collective-permute-done.1), channel_id=1, source_target_pairs={{0,1},{1,2},{2,3},{3,0},{4,5},{5,6},{6,7},{7,4},{8,9},{9,10},{10,1... | collective-permute-start | bytes 1572872 | tf_op jit(solution)/shard_map/ppermute | solution.py:14
  81.4 85.6 %copy-start.89 = (f32[256]{0:T(256)}, f32[256]{0:T(256)S(1)}, u32[]{:S(2)}) copy-start(f32[256]{0:T(256)S(1)} %get-tuple-element.555) | copy-start | bytes 3076
  81.4 85.6 %copy-start.92 = (f32[256]{0:T(256)}, f32[256]{0:T(256)S(1)}, u32[]{:S(2)}) copy-start(f32[256]{0:T(256)S(1)} %get-tuple-element.556) | copy-start | bytes 3076
  81.4 85.6 %copy-start.95 = (f32[256]{0:T(256)}, f32[256]{0:T(256)S(1)}, u32[]{:S(2)}) copy-start(f32[256]{0:T(256)S(1)} %get-tuple-element.557) | copy-start | bytes 3076
  81.4 85.6 %copy-start.98 = (f32[256]{0:T(256)}, f32[256]{0:T(256)S(1)}, u32[]{:S(2)}) copy-start(f32[256]{0:T(256)S(1)} %get-tuple-element.558) | copy-start | bytes 3076
  81.4 85.6 %copy-start.101 = (f32[256]{0:T(256)}, f32[256]{0:T(256)S(1)}, u32[]{:S(2)}) copy-start(f32[256]{0:T(256)S(1)} %get-tuple-element.559) | copy-start | bytes 3076
  81.4 85.6 %copy-start.104 = (f32[256]{0:T(256)}, f32[256]{0:T(256)S(1)}, u32[]{:S(2)}) copy-start(f32[256]{0:T(256)S(1)} %get-tuple-element.560) | copy-start | bytes 3076
  81.5 94.7 %copy-start.138 = (f32[256]{0:T(256)}, f32[256]{0:T(256)S(1)}, u32[]{:S(2)}) copy-start(f32[256]{0:T(256)S(1)} %get-tuple-element.448) | copy-start | bytes 3076
  81.5 123.2 %copy-start.108 = (f32[256]{0:T(256)}, f32[256]{0:T(256)S(1)}, u32[]{:S(2)}) copy-start(f32[256]{0:T(256)S(1)} %get-tuple-element.519) | copy-start | bytes 3076
  81.5 123.2 %copy-start.109 = (f32[256]{0:T(256)}, f32[256]{0:T(256)S(1)}, u32[]{:S(2)}) copy-start(f32[256]{0:T(256)S(1)} %get-tuple-element.520) | copy-start | bytes 3076
  81.5 126.5 %copy-start.110 = (f32[256]{0:T(256)}, f32[256]{0:T(256)S(1)}, u32[]{:S(2)}) copy-start(f32[256]{0:T(256)S(1)} %get-tuple-element.521) | copy-start | bytes 3076
  81.5 126.5 %copy-start.111 = (f32[256]{0:T(256)}, f32[256]{0:T(256)S(1)}, u32[]{:S(2)}) copy-start(f32[256]{0:T(256)S(1)} %get-tuple-element.522) | copy-start | bytes 3076
  81.5 126.5 %copy-start.112 = (f32[256]{0:T(256)}, f32[256]{0:T(256)S(1)}, u32[]{:S(2)}) copy-start(f32[256]{0:T(256)S(1)} %get-tuple-element.523) | copy-start | bytes 3076
  81.5 126.4 %copy-start.113 = (f32[256]{0:T(256)}, f32[256]{0:T(256)S(1)}, u32[]{:S(2)}) copy-start(f32[256]{0:T(256)S(1)} %get-tuple-element.524) | copy-start | bytes 3076
  81.5 126.4 %copy-start.114 = (f32[256]{0:T(256)}, f32[256]{0:T(256)S(1)}, u32[]{:S(2)}) copy-start(f32[256]{0:T(256)S(1)} %get-tuple-element.525) | copy-start | bytes 3076
  81.5 126.4 %copy-start.115 = (f32[256]{0:T(256)}, f32[256]{0:T(256)S(1)}, u32[]{:S(2)}) copy-start(f32[256]{0:T(256)S(1)} %get-tuple-element.526) | copy-start | bytes 3076
  81.5 126.4 %copy-start.116 = (f32[256]{0:T(256)}, f32[256]{0:T(256)S(1)}, u32[]{:S(2)}) copy-start(f32[256]{0:T(256)S(1)} %get-tuple-element.527) | copy-start | bytes 3076
  81.6 126.4 %copy-start.117 = (f32[256]{0:T(256)}, f32[256]{0:T(256)S(1)}, u32[]{:S(2)}) copy-start(f32[256]{0:T(256)S(1)} %get-tuple-element.528) | copy-start | bytes 3076
  81.6 129.7 %copy-start.118 = (f32[256]{0:T(256)}, f32[256]{0:T(256)S(1)}, u32[]{:S(2)}) copy-start(f32[256]{0:T(256)S(1)} %get-tuple-element.529) | copy-start | bytes 3076
  81.6 129.7 %copy-start.119 = (f32[256]{0:T(256)}, f32[256]{0:T(256)S(1)}, u32[]{:S(2)}) copy-start(f32[256]{0:T(256)S(1)} %get-tuple-element.530) | copy-start | bytes 3076
  81.6 129.7 %copy-start.120 = (f32[256]{0:T(256)}, f32[256]{0:T(256)S(1)}, u32[]{:S(2)}) copy-start(f32[256]{0:T(256)S(1)} %get-tuple-element.531) | copy-start | bytes 3076
  81.6 129.7 %copy-start.121 = (f32[256]{0:T(256)}, f32[256]{0:T(256)S(1)}, u32[]{:S(2)}) copy-start(f32[256]{0:T(256)S(1)} %get-tuple-element.532) | copy-start | bytes 3076
  81.6 129.7 %copy-start.122 = (f32[256]{0:T(256)}, f32[256]{0:T(256)S(1)}, u32[]{:S(2)}) copy-start(f32[256]{0:T(256)S(1)} %get-tuple-element.533) | copy-start | bytes 3076
  81.6 129.7 %copy-start.123 = (f32[256]{0:T(256)}, f32[256]{0:T(256)S(1)}, u32[]{:S(2)}) copy-start(f32[256]{0:T(256)S(1)} %get-tuple-element.534) | copy-start | bytes 3076
  81.6 129.7 %copy-start.124 = (f32[256]{0:T(256)}, f32[256]{0:T(256)S(1)}, u32[]{:S(2)}) copy-start(f32[256]{0:T(256)S(1)} %get-tuple-element.535) | copy-start | bytes 3076
  81.6 129.7 %copy-start.125 = (f32[256]{0:T(256)}, f32[256]{0:T(256)S(1)}, u32[]{:S(2)}) copy-start(f32[256]{0:T(256)S(1)} %get-tuple-element.536) | copy-start | bytes 3076
  81.6 133.0 %copy-start.126 = (f32[256]{0:T(256)}, f32[256]{0:T(256)S(1)}, u32[]{:S(2)}) copy-start(f32[256]{0:T(256)S(1)} %get-tuple-element.537) | copy-start | bytes 3076
  81.7 133.0 %copy-start.127 = (f32[256]{0:T(256)}, f32[256]{0:T(256)S(1)}, u32[]{:S(2)}) copy-start(f32[256]{0:T(256)S(1)} %get-tuple-element.538) | copy-start | bytes 3076
  81.7 133.0 %copy-start.128 = (f32[256]{0:T(256)}, f32[256]{0:T(256)S(1)}, u32[]{:S(2)}) copy-start(f32[256]{0:T(256)S(1)} %get-tuple-element.539) | copy-start | bytes 3076
  81.7 133.0 %copy-start.129 = (f32[256]{0:T(256)}, f32[256]{0:T(256)S(1)}, u32[]{:S(2)}) copy-start(f32[256]{0:T(256)S(1)} %get-tuple-element.540) | copy-start | bytes 3076
  81.7 133.0 %copy-start.130 = (f32[256]{0:T(256)}, f32[256]{0:T(256)S(1)}, u32[]{:S(2)}) copy-start(f32[256]{0:T(256)S(1)} %get-tuple-element.541) | copy-start | bytes 3076
  81.7 133.0 %copy-start.131 = (f32[256]{0:T(256)}, f32[256]{0:T(256)S(1)}, u32[]{:S(2)}) copy-start(f32[256]{0:T(256)S(1)} %get-tuple-element.542) | copy-start | bytes 3076
  81.7 133.0 %copy-start.132 = (f32[256]{0:T(256)}, f32[256]{0:T(256)S(1)}, u32[]{:S(2)}) copy-start(f32[256]{0:T(256)S(1)} %get-tuple-element.543) | copy-start | bytes 3076
  81.7 133.0 %copy-start.133 = (f32[256]{0:T(256)}, f32[256]{0:T(256)S(1)}, u32[]{:S(2)}) copy-start(f32[256]{0:T(256)S(1)} %get-tuple-element.544) | copy-start | bytes 3076
  81.7 136.5 %copy-start.134 = (f32[256]{0:T(256)}, f32[256]{0:T(256)S(1)}, u32[]{:S(2)}) copy-start(f32[256]{0:T(256)S(1)} %get-tuple-element.545) | copy-start | bytes 3076
  81.7 136.5 %copy-start.135 = (f32[256]{0:T(256)}, f32[256]{0:T(256)S(1)}, u32[]{:S(2)}) copy-start(f32[256]{0:T(256)S(1)} %get-tuple-element.546) | copy-start | bytes 3076
  81.7 136.5 %copy-start.136 = (f32[256]{0:T(256)}, f32[256]{0:T(256)S(1)}, u32[]{:S(2)}) copy-start(f32[256]{0:T(256)S(1)} %get-tuple-element.547) | copy-start | bytes 3076
  163.4 3.0 collective-permute-start.3
  170.9 5.0 collective-permute-start.4
  180.3 73.6 %collective-permute-start.5 = (bf16[127,1024]{1,0:T(8,128)(2,1)}, bf16[127,1024]{1,0:T(8,128)(2,1)S(1)}, u32[]{:S(2)}, u32[]{:S(2)}) collective-permute-start(bf16[127,1024]{1,0:T(8,128)(2,1)} %slice.2608), channel_id=1, source_target_pairs={{4,0},{8,4},{12,8},{16,12},{20,16},{24,20},{28,24},{5,1},{9,5},{13... | collective-permute-start | bytes 780296 | tf_op jit(solution)/shard_map/ppermute | solution.py:27
  293.1 72.3 %collective-permute-start.6 = (bf16[6,3,1024]{2,0,1:T(8,128)(2,1)S(1)}, bf16[6,3,1024]{2,0,1:T(8,128)(2,1)S(1)}, u32[]{:S(2)}, u32[]{:S(2)}) collective-permute-start(bf16[6,3,1024]{2,0,1:T(8,128)(2,1)S(1)} %slice.2737), channel_id=1, source_target_pairs={{4,0},{8,4},{12,8},{16,12},{20,16},{24,20},{28,24},{5,1},{9,5},{13... | collective-permute-start | bytes 110600 | tf_op jit(solution)/shard_map/ppermute | solution.py:27
  365.4 108.8 %reduce-scatter.3.cloned.1.call-start = ((), (), s32[]{:S(2)}) async-start(), calls=%async_computation.4 | async-start | bytes 2621440 | tf_op jit(solution)/shard_map/reduce_scatter | solution.py:147
  383.0 251.5 %reduce-scatter.5.cloned.1.call-start = ((), (), s32[]{:S(2)}) async-start(), calls=%async_computation.5 | async-start | bytes 28311552 | tf_op jit(solution)/shard_map/reduce_scatter | solution.py:150
  (149 other events, 3189.3 us)
Sparse Core Ops, SparseCore 0:
  9.9 141.2 all-gather.1
  365.5 62.3 all-reduce.1
  430.9 43.2 reduce-scatter.2
  478.2 156.1 reduce-scatter.4
